TPU v7x, 256 devices: a whole 4x4x8 slice. The times are simulated.
256 devices in a mesh: tx: 16 (over z, core), gx: 8 (over x, y_lo), gy: 2 (over y_hi).
Axes of the slice: x: 4, y: 4 (y_hi: 2, y_lo: 2; y = y_hi * 2 + y_lo), z: 8, core: 2. Of those that a mesh axis runs over, the one named last changes fastest.
Arguments:
- cond_h: float32 [128, 32, 128], P('gx', 'gy'), may hold values from 0.1 to 1.5
- cond_v: float32 [128, 32, 128], P('gx', 'gy'), may hold values from 0.1 to 1.5
- fwd_init: float32 [16, 6, 128, 32, 128], P('tx', None, 'gx', 'gy'), may hold values from -6 to 6
- adj_init: float32 [16, 6, 128, 32, 128], P('tx', None, 'gx', 'gy'), may hold values from -6 to 6
- observed: float32 [16, 4, 8, 2, 2, 32], P('tx', None, 'gx', 'gy'), may hold values from -6 to 6
- footprint: int32 [16, 8, 2], P('tx', 'gx', 'gy'), may hold values 0 or 1
- owner: int32 [8, 2, 16], P('gx', 'gy'), may hold values from 0 to 15, each once within a row
- rec_cells: int32 [8, 2, 32], P('gx', 'gy'), may hold values from 0 to 255
Outputs:
- owned_gradient: float32 [8, 16, 2, 1, 32, 128], P('gx', 'tx', None, None, 'gy')
- misfit: float32 [], replicated
Inputs may be any that keep to these rules, and one draw needn't show every extreme that they name: `owner`: each tile's row is a permutation of 0 to 15. `rec_cells`: cell index x * 16 + y within the tile; receivers may share a cell. `footprint`: 1 where the group's gradient counts in the tile.
All inputs are finite; a program needn't handle non-finite values.
Results may differ from a plain program's by a relative error of at most 0.00028.
Values sent between devices are 32-bit elements; how exact they have to be, the bound alone decides.
No kernel may reach another device: no remote copies, remote signals or barrier semaphores. Data moves between devices by JAX's collectives and lax.ppermute only.
A program may use at most 64 MiB of HBM per device.

v0:
```python
import jax
import jax.numpy as jnp
from jax import lax
from jax.sharding import PartitionSpec as P

STEPS = 4
ZREC = 32
STEP_DT = 0.5


def shifted(x, axis, by):
    size = lax.axis_size(axis)
    pairs = [(i, i + by) for i in range(size) if 0 <= i + by < size]
    return lax.ppermute(x, axis, pairs)


def coefficients(conduct):
    half_rate = 0.25 * conduct
    return ((1.0 - half_rate) / (1.0 + half_rate), STEP_DT / (1.0 + half_rate))


def ahead_of(values, tail_plane, axis_num):
    extent = values.shape[axis_num]
    return jnp.concatenate(
        [lax.slice_in_dim(values, 1, extent, axis=axis_num), tail_plane], axis=axis_num
    )


def before(values, head_plane, axis_num):
    extent = values.shape[axis_num]
    return jnp.concatenate(
        [head_plane, lax.slice_in_dim(values, 0, extent - 1, axis=axis_num)], axis=axis_num
    )


def zero_plane(values, axis_num):
    return jnp.zeros_like(lax.slice_in_dim(values, 0, 1, axis=axis_num))


def curl_ahead(field, next_x, next_y):
    comp_x, comp_y, comp_z = (field[0], field[1], field[2])
    out_x = (
        ahead_of(comp_z, next_y[1], 1)
        - comp_z
        - (ahead_of(comp_y, zero_plane(comp_y, 2), 2) - comp_y)
    )
    out_y = (
        ahead_of(comp_x, zero_plane(comp_x, 2), 2)
        - comp_x
        - (ahead_of(comp_z, next_x[1], 0) - comp_z)
    )
    out_z = ahead_of(comp_y, next_x[0], 0) - comp_y - (ahead_of(comp_x, next_y[0], 1) - comp_x)
    return jnp.stack([out_x, out_y, out_z])


def curl_before(field, prev_x, prev_y):
    comp_x, comp_y, comp_z = (field[0], field[1], field[2])
    out_x = (
        comp_z - before(comp_z, prev_y[1], 1) - (comp_y - before(comp_y, zero_plane(comp_y, 2), 2))
    )
    out_y = (
        comp_x - before(comp_x, zero_plane(comp_x, 2), 2) - (comp_z - before(comp_z, prev_x[1], 0))
    )
    out_z = comp_y - before(comp_y, prev_x[0], 0) - (comp_x - before(comp_x, prev_y[0], 1))
    return jnp.stack([out_x, out_y, out_z])


def electric_rims(electric):
    next_x = shifted(electric[1:3, 0:1], "gx", -1)
    next_y = shifted(electric[0::2, :, 0:1], "gy", -1)
    return (next_x, next_y)


def magnetic_rims(magnetic):
    size_x = magnetic.shape[1]
    size_y = magnetic.shape[2]
    prev_x = shifted(magnetic[1:3, size_x - 1 : size_x], "gx", 1)
    prev_y = shifted(magnetic[0::2, :, size_y - 1 : size_y], "gy", 1)
    return (prev_x, prev_y)


def advance(electric, magnetic, decay, drive):
    next_x, next_y = electric_rims(electric)
    magnetic = magnetic - STEP_DT * curl_ahead(electric, next_x, next_y)
    prev_x, prev_y = magnetic_rims(magnetic)
    electric = decay * electric + drive * curl_before(magnetic, prev_x, prev_y)
    return (electric, magnetic)


def on_device(cond_h, cond_v, fwd_init, adj_init, observed, footprint, owner, rec_cells):
    size_x, size_y, depth = cond_h.shape
    decay_h, drive_h = coefficients(cond_h)
    decay_v, drive_v = coefficients(cond_v)
    highest = lax.Precision.HIGHEST
    cell_ids = jnp.arange(size_x * size_y, dtype=jnp.int32)
    onehot = (rec_cells[0, 0][:, None] == cell_ids[None, :]).astype(jnp.float32)
    observe = observed[0, :, 0, 0]
    grad_h = jnp.zeros((size_x, size_y, depth), jnp.float32)
    grad_v = jnp.zeros((size_x, size_y, depth), jnp.float32)
    residuals = []
    decay = jnp.stack([decay_h, decay_h, decay_v])
    drive = jnp.stack([drive_h, drive_h, drive_v])
    electric, magnetic = (fwd_init[0, 0:3], fwd_init[0, 3:6])
    stored = []
    for step_idx in range(STEPS):
        electric, magnetic = advance(electric, magnetic, decay, drive)
        stored.append(electric)
        planes = electric[0:2, :, :, ZREC].reshape(2, size_x * size_y)
        residuals.append(jnp.dot(planes, onehot.T, precision=highest) - observe[step_idx])
    adj_e, adj_h = (adj_init[0, 0:3], adj_init[0, 3:6])
    for step_idx in reversed(range(STEPS)):
        adj_e = adj_e.at[0:2, :, :, ZREC].add(
            jnp.dot(residuals[step_idx], onehot, precision=highest).reshape(2, size_x, size_y)
        )
        adj_e, adj_h = advance(adj_e, adj_h, decay, drive)
        kept = stored[step_idx]
        grad_h = grad_h + adj_e[0] * kept[0] + adj_e[1] * kept[1]
        grad_v = grad_v + adj_e[2] * kept[2]
    local_misfit = jnp.float32(0.0)
    for step_idx in range(STEPS):
        local_misfit = local_misfit + 0.5 * jnp.sum(residuals[step_idx] * residuals[step_idx])
    misfit = lax.psum(local_misfit, ("tx", "gx", "gy"))
    tile_flag = footprint[0, 0, 0].astype(jnp.float32)
    gradient = jnp.stack([grad_h, grad_v]) * tile_flag
    groups_count = lax.axis_size("tx")
    block_rows = size_x // groups_count
    blocked = gradient.reshape(2, groups_count, block_rows, size_y, depth)
    ordered = jnp.take(blocked, owner[0, 0], axis=1)
    summed = lax.psum_scatter(ordered, "tx", scatter_dimension=1, tiled=True)
    owned_part = summed.reshape(1, 1, 2, block_rows, size_y, depth)
    return (owned_part, misfit)


def solution(mesh):
    placed = (
        P("gx", "gy", None),
        P("gx", "gy", None),
        P("tx", None, "gx", "gy", None),
        P("tx", None, "gx", "gy", None),
        P("tx", None, "gx", "gy", None, None),
        P("tx", "gx", "gy"),
        P("gx", "gy", None),
        P("gx", "gy", None),
    )
    return jax.shard_map(
        on_device,
        mesh=mesh,
        in_specs=placed,
        out_specs=(P("gx", "tx", None, None, "gy", None), P()),
        check_vma=False,
    )
```

profile of v0, /device:TPU:1, one launch (start us, length us, event | category | flops | bytes accessed | tf_op | source)
XLA Modules:
  0.0 326.6 jit_solution(11279298193173657843)
XLA Ops:
  15.4 2.0 and_reduce_fusion
  19.2 5.6 %collective-permute-start.2 = (f32[2,16,1,128]{3,1,2,0:T(8,128)S(1)}, f32[2,16,1,128]{3,1,2,0:T(8,128)S(1)}, u32[]{:S(2)}, u32[]{:S(2)}) collective-permute-start(f32[2,16,1,128]{3,1,2,0:T(8,128)S(1)} %bitcast.592), channel_id=1, source_target_pairs={{0,1},{2,3},{4,5},{6,7},{8,9},{10,11},{12,13},{14,15},{16,17},{18,... | collective-permute-start | bytes 49160 | tf_op jit(solution)/shard_map/ppermute | solution.py:14
  24.9 4.5 %collective-permute-start.3 = (f32[2,1,16,128]{3,2,1,0:T(8,128)S(1)}, f32[2,1,16,128]{3,2,1,0:T(8,128)S(1)}, u32[]{:S(2)}, u32[]{:S(2)}) collective-permute-start(f32[2,1,16,128]{3,2,1,0:T(8,128)S(1)} %slice.1340), channel_id=1, source_target_pairs={{0,2},{2,4},{4,6},{6,8},{8,10},{10,12},{12,14},{1,3},{3,5},{5,7},{... | collective-permute-start | bytes 49160 | tf_op jit(solution)/shard_map/ppermute | solution.py:14
  41.6 6.1 %collective-permute-start.6 = (f32[2,16,1,128]{3,1,2,0:T(8,128)S(1)}, f32[2,16,1,128]{3,1,2,0:T(8,128)S(1)}, u32[]{:S(2)}, u32[]{:S(2)}) collective-permute-start(f32[2,16,1,128]{3,1,2,0:T(8,128)S(1)} %bitcast.593), channel_id=1, source_target_pairs={{0,1},{2,3},{4,5},{6,7},{8,9},{10,11},{12,13},{14,15},{16,17},{18,... | collective-permute-start | bytes 49160 | tf_op jit(solution)/shard_map/ppermute | solution.py:14
  47.8 3.7 %collective-permute-start.7 = (f32[2,1,16,128]{3,2,1,0:T(8,128)S(1)}, f32[2,1,16,128]{3,2,1,0:T(8,128)S(1)}, u32[]{:S(2)}, u32[]{:S(2)}) collective-permute-start(f32[2,1,16,128]{3,2,1,0:T(8,128)S(1)} %slice.1368), channel_id=1, source_target_pairs={{0,2},{2,4},{4,6},{6,8},{8,10},{10,12},{12,14},{1,3},{3,5},{5,7},{... | collective-permute-start | bytes 49160 | tf_op jit(solution)/shard_map/ppermute | solution.py:14
  56.2 1.6 multiply_reduce_fusion.2
  61.5 2.3 collective-permute-done.8
  68.3 6.1 %collective-permute-start.10 = (f32[2,16,1,128]{3,1,2,0:T(8,128)S(1)}, f32[2,16,1,128]{3,1,2,0:T(8,128)S(1)}, u32[]{:S(2)}, u32[]{:S(2)}) collective-permute-start(f32[2,16,1,128]{3,1,2,0:T(8,128)S(1)} %bitcast.594), channel_id=1, source_target_pairs={{0,1},{2,3},{4,5},{6,7},{8,9},{10,11},{12,13},{14,15},{16,17},{18,... | collective-permute-start | bytes 49160 | tf_op jit(solution)/shard_map/ppermute | solution.py:14
  74.5 3.7 %collective-permute-start.11 = (f32[2,1,16,128]{3,2,1,0:T(8,128)S(1)}, f32[2,1,16,128]{3,2,1,0:T(8,128)S(1)}, u32[]{:S(2)}, u32[]{:S(2)}) collective-permute-start(f32[2,1,16,128]{3,2,1,0:T(8,128)S(1)} %slice.1396), channel_id=1, source_target_pairs={{0,2},{2,4},{4,6},{6,8},{8,10},{10,12},{12,14},{1,3},{3,5},{5,7},{... | collective-permute-start | bytes 49160 | tf_op jit(solution)/shard_map/ppermute | solution.py:14
  97.4 5.9 %collective-permute-start.14 = (f32[2,16,1,128]{3,1,2,0:T(8,128)S(1)}, f32[2,16,1,128]{3,1,2,0:T(8,128)S(1)}, u32[]{:S(2)}, u32[]{:S(2)}) collective-permute-start(f32[2,16,1,128]{3,1,2,0:T(8,128)S(1)} %bitcast.595), channel_id=1, source_target_pairs={{0,1},{2,3},{4,5},{6,7},{8,9},{10,11},{12,13},{14,15},{16,17},{18,... | collective-permute-start | bytes 49160 | tf_op jit(solution)/shard_map/ppermute | solution.py:14
  103.3 3.7 %collective-permute-start.15 = (f32[2,1,16,128]{3,2,1,0:T(8,128)S(1)}, f32[2,1,16,128]{3,2,1,0:T(8,128)S(1)}, u32[]{:S(2)}, u32[]{:S(2)}) collective-permute-start(f32[2,1,16,128]{3,2,1,0:T(8,128)S(1)} %slice.1424), channel_id=1, source_target_pairs={{0,2},{2,4},{4,6},{6,8},{8,10},{10,12},{12,14},{1,3},{3,5},{5,7},{... | collective-permute-start | bytes 49160 | tf_op jit(solution)/shard_map/ppermute | solution.py:14
  112.3 2.0 add_select_fusion.3
  114.3 3.6 %scatter-add.14 = f32[3,16,16,128]{3,2,1,0:T(8,128)S(1)} dynamic-update-slice(f32[3,16,16,128]{3,2,1,0:T(8,128)S(1)} %get-tuple-element.51, f32[2,16,16,1]{3,2,1,0:T(8,128)S(1)} %add_select_fusion.3, s32[]{:T(128)} %bitcast.4, s32[]{:T(128)} %constant.106.clone.1, s32[]{:T(128)} %constant.106.clone.1, s32[]{:T(128)} %bitcast.5) | dynamic-update-slice | bytes 4100 | tf_op jit(solution)/shard_map/scatter-add | solution.py:112
  120.7 3.3 collective-permute-done.16
  126.3 6.1 %collective-permute-start.18 = (f32[2,16,1,128]{3,1,2,0:T(8,128)S(1)}, f32[2,16,1,128]{3,1,2,0:T(8,128)S(1)}, u32[]{:S(2)}, u32[]{:S(2)}) collective-permute-start(f32[2,16,1,128]{3,1,2,0:T(8,128)S(1)} %bitcast.596), channel_id=1, source_target_pairs={{0,1},{2,3},{4,5},{6,7},{8,9},{10,11},{12,13},{14,15},{16,17},{18,... | collective-permute-start | bytes 49160 | tf_op jit(solution)/shard_map/ppermute | solution.py:14
  132.4 3.7 %collective-permute-start.19 = (f32[2,1,16,128]{3,2,1,0:T(8,128)S(1)}, f32[2,1,16,128]{3,2,1,0:T(8,128)S(1)}, u32[]{:S(2)}, u32[]{:S(2)}) collective-permute-start(f32[2,1,16,128]{3,2,1,0:T(8,128)S(1)} %slice.1453), channel_id=1, source_target_pairs={{0,2},{2,4},{4,6},{6,8},{8,10},{10,12},{12,14},{1,3},{3,5},{5,7},{... | collective-permute-start | bytes 49160 | tf_op jit(solution)/shard_map/ppermute | solution.py:14
  138.2 2.0 add_select_fusion.2
  140.3 3.6 %scatter-add.15 = f32[3,16,16,128]{3,2,1,0:T(8,128)S(1)} dynamic-update-slice(f32[3,16,16,128]{3,2,1,0:T(8,128)S(1)} %copy.87, f32[2,16,16,1]{3,2,1,0:T(8,128)S(1)} %add_select_fusion.2, s32[]{:T(128)} %bitcast.4, s32[]{:T(128)} %constant.106.clone.1, s32[]{:T(128)} %constant.106.clone.1, s32[]{:T(128)} %bitcast.5) | dynamic-update-slice | bytes 4100 | tf_op jit(solution)/shard_map/scatter-add | solution.py:112
  146.7 3.3 collective-permute-done.20
  151.7 6.1 %collective-permute-start.22 = (f32[2,16,1,128]{3,1,2,0:T(8,128)S(1)}, f32[2,16,1,128]{3,1,2,0:T(8,128)S(1)}, u32[]{:S(2)}, u32[]{:S(2)}) collective-permute-start(f32[2,16,1,128]{3,1,2,0:T(8,128)S(1)} %bitcast.597), channel_id=1, source_target_pairs={{0,1},{2,3},{4,5},{6,7},{8,9},{10,11},{12,13},{14,15},{16,17},{18,... | collective-permute-start | bytes 49160 | tf_op jit(solution)/shard_map/ppermute | solution.py:14
  157.8 3.7 %collective-permute-start.23 = (f32[2,1,16,128]{3,2,1,0:T(8,128)S(1)}, f32[2,1,16,128]{3,2,1,0:T(8,128)S(1)}, u32[]{:S(2)}, u32[]{:S(2)}) collective-permute-start(f32[2,1,16,128]{3,2,1,0:T(8,128)S(1)} %slice.1486), channel_id=1, source_target_pairs={{0,2},{2,4},{4,6},{6,8},{8,10},{10,12},{12,14},{1,3},{3,5},{5,7},{... | collective-permute-start | bytes 49160 | tf_op jit(solution)/shard_map/ppermute | solution.py:14
  163.6 2.0 add_select_fusion.1
  165.6 3.6 %scatter-add.16 = f32[3,16,16,128]{3,2,1,0:T(8,128)S(1)} dynamic-update-slice(f32[3,16,16,128]{3,2,1,0:T(8,128)S(1)} %copy.88, f32[2,16,16,1]{3,2,1,0:T(8,128)S(1)} %add_select_fusion.1, s32[]{:T(128)} %bitcast.4, s32[]{:T(128)} %constant.106.clone.1, s32[]{:T(128)} %constant.106.clone.1, s32[]{:T(128)} %bitcast.5) | dynamic-update-slice | bytes 4100 | tf_op jit(solution)/shard_map/scatter-add | solution.py:112
  172.2 3.1 collective-permute-done.24
  177.5 6.1 %collective-permute-start.26 = (f32[2,16,1,128]{3,1,2,0:T(8,128)S(1)}, f32[2,16,1,128]{3,1,2,0:T(8,128)S(1)}, u32[]{:S(2)}, u32[]{:S(2)}) collective-permute-start(f32[2,16,1,128]{3,1,2,0:T(8,128)S(1)} %bitcast.598), channel_id=1, source_target_pairs={{0,1},{2,3},{4,5},{6,7},{8,9},{10,11},{12,13},{14,15},{16,17},{18,... | collective-permute-start | bytes 49160 | tf_op jit(solution)/shard_map/ppermute | solution.py:14
  183.6 3.7 %collective-permute-start.27 = (f32[2,1,16,128]{3,2,1,0:T(8,128)S(1)}, f32[2,1,16,128]{3,2,1,0:T(8,128)S(1)}, u32[]{:S(2)}, u32[]{:S(2)}) collective-permute-start(f32[2,1,16,128]{3,2,1,0:T(8,128)S(1)} %slice.1517), channel_id=1, source_target_pairs={{0,2},{2,4},{4,6},{6,8},{8,10},{10,12},{12,14},{1,3},{3,5},{5,7},{... | collective-permute-start | bytes 49160 | tf_op jit(solution)/shard_map/ppermute | solution.py:14
  189.6 2.0 add_select_fusion
  191.6 3.6 %scatter-add.19 = f32[3,16,16,128]{3,2,1,0:T(8,128)S(1)} dynamic-update-slice(f32[3,16,16,128]{3,2,1,0:T(8,128)S(1)} %copy.89, f32[2,16,16,1]{3,2,1,0:T(8,128)S(1)} %add_select_fusion, s32[]{:T(128)} %bitcast.4, s32[]{:T(128)} %constant.106.clone.1, s32[]{:T(128)} %constant.106.clone.1, s32[]{:T(128)} %bitcast.5) | dynamic-update-slice | bytes 4100 | tf_op jit(solution)/shard_map/scatter-add | solution.py:112
  198.0 3.3 collective-permute-done.28
  203.1 6.1 %collective-permute-start.30 = (f32[2,16,1,128]{3,1,2,0:T(8,128)S(1)}, f32[2,16,1,128]{3,1,2,0:T(8,128)S(1)}, u32[]{:S(2)}, u32[]{:S(2)}) collective-permute-start(f32[2,16,1,128]{3,1,2,0:T(8,128)S(1)} %bitcast.599), channel_id=1, source_target_pairs={{0,1},{2,3},{4,5},{6,7},{8,9},{10,11},{12,13},{14,15},{16,17},{18,... | collective-permute-start | bytes 49160 | tf_op jit(solution)/shard_map/ppermute | solution.py:14
  209.3 3.7 %collective-permute-start.31 = (f32[2,1,16,128]{3,2,1,0:T(8,128)S(1)}, f32[2,1,16,128]{3,2,1,0:T(8,128)S(1)}, u32[]{:S(2)}, u32[]{:S(2)}) collective-permute-start(f32[2,1,16,128]{3,2,1,0:T(8,128)S(1)} %slice.1548), channel_id=1, source_target_pairs={{0,2},{2,4},{4,6},{6,8},{8,10},{10,12},{12,14},{1,3},{3,5},{5,7},{... | collective-permute-start | bytes 49160 | tf_op jit(solution)/shard_map/ppermute | solution.py:14
  219.5 100.3 %psum.7 = f32[]{:T(128)} all-reduce(f32[]{:T(128)S(6)} %add.229), channel_id=1, replica_groups=mesh['tx'=16,'gx'=8,'gy'=2] {'tx','gx','gy'}, use_global_device_ids=true, to_apply=%region_6.0 | all-reduce | flops 1 | bytes 8 | tf_op jit(solution)/shard_map/psum | solution.py:122
  (429 shorter events, 87.6 us)
Async XLA Ops:
  7.2 312.6 %reduce-scatter.2.cloned.1.call-start = ((), (), s32[]{:S(2)}) async-start(), calls=%async_computation.1 | async-start | bytes 278528 | tf_op jit(solution)/shard_map/reduce_scatter | solution.py:129
  8.3 10.5 %collective-permute-start = (f32[2,16,1,128]{3,2,1,0:T(1,128)S(1)}, f32[2,16,1,128]{3,2,1,0:T(1,128)S(1)}, u32[]{:S(2)}, u32[]{:S(2)}) collective-permute-start(f32[2,16,1,128]{3,2,1,0:T(1,128)S(1)} %slice.1044), channel_id=1, source_target_pairs={{1,0},{3,2},{5,4},{7,6},{9,8},{11,10},{13,12},{15,14},{17,16},{19,... | collective-permute-start | bytes 49160 | tf_op jit(solution)/shard_map/ppermute | solution.py:14
  9.6 9.2 %collective-permute-start.1 = (f32[2,1,16,128]{3,2,1,0:T(8,128)S(1)}, f32[2,1,16,128]{3,2,1,0:T(8,128)S(1)}, u32[]{:S(2)}, u32[]{:S(2)}) collective-permute-start(f32[2,1,16,128]{3,2,1,0:T(8,128)S(1)} %slice.1328), channel_id=1, source_target_pairs={{2,0},{4,2},{6,4},{8,6},{10,8},{12,10},{14,12},{3,1},{5,3},{7,5},{... | collective-permute-start | bytes 49160 | tf_op jit(solution)/shard_map/ppermute | solution.py:14
  19.2 10.2 %collective-permute-start.2 = (f32[2,16,1,128]{3,1,2,0:T(8,128)S(1)}, f32[2,16,1,128]{3,1,2,0:T(8,128)S(1)}, u32[]{:S(2)}, u32[]{:S(2)}) collective-permute-start(f32[2,16,1,128]{3,1,2,0:T(8,128)S(1)} %bitcast.592), channel_id=1, source_target_pairs={{0,1},{2,3},{4,5},{6,7},{8,9},{10,11},{12,13},{14,15},{16,17},{18,... | collective-permute-start | bytes 49160 | tf_op jit(solution)/shard_map/ppermute | solution.py:14
  24.9 5.4 %collective-permute-start.3 = (f32[2,1,16,128]{3,2,1,0:T(8,128)S(1)}, f32[2,1,16,128]{3,2,1,0:T(8,128)S(1)}, u32[]{:S(2)}, u32[]{:S(2)}) collective-permute-start(f32[2,1,16,128]{3,2,1,0:T(8,128)S(1)} %slice.1340), channel_id=1, source_target_pairs={{0,2},{2,4},{4,6},{6,8},{8,10},{10,12},{12,14},{1,3},{3,5},{5,7},{... | collective-permute-start | bytes 49160 | tf_op jit(solution)/shard_map/ppermute | solution.py:14
  32.5 6.0 %collective-permute-start.4 = (f32[2,16,1,128]{3,2,1,0:T(1,128)S(1)}, f32[2,16,1,128]{3,2,1,0:T(1,128)S(1)}, u32[]{:S(2)}, u32[]{:S(2)}) collective-permute-start(f32[2,16,1,128]{3,2,1,0:T(1,128)S(1)} %slice.1076), channel_id=1, source_target_pairs={{1,0},{3,2},{5,4},{7,6},{9,8},{11,10},{13,12},{15,14},{17,16},{19,... | collective-permute-start | bytes 49160 | tf_op jit(solution)/shard_map/ppermute | solution.py:14
  33.8 6.0 %collective-permute-start.5 = (f32[2,1,16,128]{3,2,1,0:T(8,128)S(1)}, f32[2,1,16,128]{3,2,1,0:T(8,128)S(1)}, u32[]{:S(2)}, u32[]{:S(2)}) collective-permute-start(f32[2,1,16,128]{3,2,1,0:T(8,128)S(1)} %slice.1355), channel_id=1, source_target_pairs={{2,0},{4,2},{6,4},{8,6},{10,8},{12,10},{14,12},{3,1},{5,3},{7,5},{... | collective-permute-start | bytes 49160 | tf_op jit(solution)/shard_map/ppermute | solution.py:14
  41.6 9.8 %collective-permute-start.6 = (f32[2,16,1,128]{3,1,2,0:T(8,128)S(1)}, f32[2,16,1,128]{3,1,2,0:T(8,128)S(1)}, u32[]{:S(2)}, u32[]{:S(2)}) collective-permute-start(f32[2,16,1,128]{3,1,2,0:T(8,128)S(1)} %bitcast.593), channel_id=1, source_target_pairs={{0,1},{2,3},{4,5},{6,7},{8,9},{10,11},{12,13},{14,15},{16,17},{18,... | collective-permute-start | bytes 49160 | tf_op jit(solution)/shard_map/ppermute | solution.py:14
  47.8 4.5 %collective-permute-start.7 = (f32[2,1,16,128]{3,2,1,0:T(8,128)S(1)}, f32[2,1,16,128]{3,2,1,0:T(8,128)S(1)}, u32[]{:S(2)}, u32[]{:S(2)}) collective-permute-start(f32[2,1,16,128]{3,2,1,0:T(8,128)S(1)} %slice.1368), channel_id=1, source_target_pairs={{0,2},{2,4},{4,6},{6,8},{8,10},{10,12},{12,14},{1,3},{3,5},{5,7},{... | collective-permute-start | bytes 49160 | tf_op jit(solution)/shard_map/ppermute | solution.py:14
  57.8 6.0 %collective-permute-start.8 = (f32[2,16,1,128]{3,2,1,0:T(1,128)S(1)}, f32[2,16,1,128]{3,2,1,0:T(1,128)S(1)}, u32[]{:S(2)}, u32[]{:S(2)}) collective-permute-start(f32[2,16,1,128]{3,2,1,0:T(1,128)S(1)} %copy-done.74), channel_id=1, source_target_pairs={{1,0},{3,2},{5,4},{7,6},{9,8},{11,10},{13,12},{15,14},{17,16},{19,... | collective-permute-start | bytes 49160 | tf_op jit(solution)/shard_map/ppermute | solution.py:14
  59.1 5.9 %collective-permute-start.9 = (f32[2,1,16,128]{3,2,1,0:T(8,128)S(1)}, f32[2,1,16,128]{3,2,1,0:T(8,128)S(1)}, u32[]{:S(2)}, u32[]{:S(2)}) collective-permute-start(f32[2,1,16,128]{3,2,1,0:T(8,128)S(1)} %copy-done.72), channel_id=1, source_target_pairs={{2,0},{4,2},{6,4},{8,6},{10,8},{12,10},{14,12},{3,1},{5,3},{7,5},{... | collective-permute-start | bytes 49160 | tf_op jit(solution)/shard_map/ppermute | solution.py:14
  68.3 9.8 %collective-permute-start.10 = (f32[2,16,1,128]{3,1,2,0:T(8,128)S(1)}, f32[2,16,1,128]{3,1,2,0:T(8,128)S(1)}, u32[]{:S(2)}, u32[]{:S(2)}) collective-permute-start(f32[2,16,1,128]{3,1,2,0:T(8,128)S(1)} %bitcast.594), channel_id=1, source_target_pairs={{0,1},{2,3},{4,5},{6,7},{8,9},{10,11},{12,13},{14,15},{16,17},{18,... | collective-permute-start | bytes 49160 | tf_op jit(solution)/shard_map/ppermute | solution.py:14
  74.5 4.5 %collective-permute-start.11 = (f32[2,1,16,128]{3,2,1,0:T(8,128)S(1)}, f32[2,1,16,128]{3,2,1,0:T(8,128)S(1)}, u32[]{:S(2)}, u32[]{:S(2)}) collective-permute-start(f32[2,1,16,128]{3,2,1,0:T(8,128)S(1)} %slice.1396), channel_id=1, source_target_pairs={{0,2},{2,4},{4,6},{6,8},{8,10},{10,12},{12,14},{1,3},{3,5},{5,7},{... | collective-permute-start | bytes 49160 | tf_op jit(solution)/shard_map/ppermute | solution.py:14
  86.1 6.4 %collective-permute-start.12 = (f32[2,16,1,128]{3,1,2,0:T(8,128)}, f32[2,16,1,128]{3,1,2,0:T(8,128)}, u32[]{:S(2)}, u32[]{:S(2)}) collective-permute-start(f32[2,16,1,128]{3,1,2,0:T(8,128)} %bitcast.197), channel_id=1, source_target_pairs={{1,0},{3,2},{5,4},{7,6},{9,8},{11,10},{13,12},{15,14},{17,16},{19,... | collective-permute-start | bytes 49160 | tf_op jit(solution)/shard_map/ppermute | solution.py:14
  87.5 5.7 %collective-permute-start.13 = (f32[2,1,16,128]{3,2,1,0:T(8,128)S(1)}, f32[2,1,16,128]{3,2,1,0:T(8,128)}, u32[]{:S(2)}, u32[]{:S(2)}) collective-permute-start(f32[2,1,16,128]{3,2,1,0:T(8,128)S(1)} %copy-done.73), channel_id=1, source_target_pairs={{2,0},{4,2},{6,4},{8,6},{10,8},{12,10},{14,12},{3,1},{5,3},{7,5},{... | collective-permute-start | bytes 49160 | tf_op jit(solution)/shard_map/ppermute | solution.py:14
  97.4 9.6 %collective-permute-start.14 = (f32[2,16,1,128]{3,1,2,0:T(8,128)S(1)}, f32[2,16,1,128]{3,1,2,0:T(8,128)S(1)}, u32[]{:S(2)}, u32[]{:S(2)}) collective-permute-start(f32[2,16,1,128]{3,1,2,0:T(8,128)S(1)} %bitcast.595), channel_id=1, source_target_pairs={{0,1},{2,3},{4,5},{6,7},{8,9},{10,11},{12,13},{14,15},{16,17},{18,... | collective-permute-start | bytes 49160 | tf_op jit(solution)/shard_map/ppermute | solution.py:14
  103.3 4.5 %collective-permute-start.15 = (f32[2,1,16,128]{3,2,1,0:T(8,128)S(1)}, f32[2,1,16,128]{3,2,1,0:T(8,128)S(1)}, u32[]{:S(2)}, u32[]{:S(2)}) collective-permute-start(f32[2,1,16,128]{3,2,1,0:T(8,128)S(1)} %slice.1424), channel_id=1, source_target_pairs={{0,2},{2,4},{4,6},{6,8},{8,10},{10,12},{12,14},{1,3},{3,5},{5,7},{... | collective-permute-start | bytes 49160 | tf_op jit(solution)/shard_map/ppermute | solution.py:14
  118.0 6.0 %collective-permute-start.16 = (f32[2,16,1,128]{3,1,2,0:T(8,128)S(1)}, f32[2,16,1,128]{3,1,2,0:T(8,128)S(1)}, u32[]{:S(2)}, u32[]{:S(2)}) collective-permute-start(f32[2,16,1,128]{3,1,2,0:T(8,128)S(1)} %bitcast.589), channel_id=1, source_target_pairs={{1,0},{3,2},{5,4},{7,6},{9,8},{11,10},{13,12},{15,14},{17,16},{19,... | collective-permute-start | bytes 49160 | tf_op jit(solution)/shard_map/ppermute | solution.py:14
  119.4 5.5 %collective-permute-start.17 = (f32[2,1,16,128]{3,2,1,0:T(8,128)S(1)}, f32[2,1,16,128]{3,2,1,0:T(8,128)S(1)}, u32[]{:S(2)}, u32[]{:S(2)}) collective-permute-start(f32[2,1,16,128]{3,2,1,0:T(8,128)S(1)} %slice.1440), channel_id=1, source_target_pairs={{2,0},{4,2},{6,4},{8,6},{10,8},{12,10},{14,12},{3,1},{5,3},{7,5},{... | collective-permute-start | bytes 49160 | tf_op jit(solution)/shard_map/ppermute | solution.py:14
  126.3 9.8 %collective-permute-start.18 = (f32[2,16,1,128]{3,1,2,0:T(8,128)S(1)}, f32[2,16,1,128]{3,1,2,0:T(8,128)S(1)}, u32[]{:S(2)}, u32[]{:S(2)}) collective-permute-start(f32[2,16,1,128]{3,1,2,0:T(8,128)S(1)} %bitcast.596), channel_id=1, source_target_pairs={{0,1},{2,3},{4,5},{6,7},{8,9},{10,11},{12,13},{14,15},{16,17},{18,... | collective-permute-start | bytes 49160 | tf_op jit(solution)/shard_map/ppermute | solution.py:14
  132.4 4.5 %collective-permute-start.19 = (f32[2,1,16,128]{3,2,1,0:T(8,128)S(1)}, f32[2,1,16,128]{3,2,1,0:T(8,128)S(1)}, u32[]{:S(2)}, u32[]{:S(2)}) collective-permute-start(f32[2,1,16,128]{3,2,1,0:T(8,128)S(1)} %slice.1453), channel_id=1, source_target_pairs={{0,2},{2,4},{4,6},{6,8},{8,10},{10,12},{12,14},{1,3},{3,5},{5,7},{... | collective-permute-start | bytes 49160 | tf_op jit(solution)/shard_map/ppermute | solution.py:14
  143.9 6.0 %collective-permute-start.20 = (f32[2,16,1,128]{3,1,2,0:T(8,128)S(1)}, f32[2,16,1,128]{3,1,2,0:T(8,128)S(1)}, u32[]{:S(2)}, u32[]{:S(2)}) collective-permute-start(f32[2,16,1,128]{3,1,2,0:T(8,128)S(1)} %bitcast.590), channel_id=1, source_target_pairs={{1,0},{3,2},{5,4},{7,6},{9,8},{11,10},{13,12},{15,14},{17,16},{19,... | collective-permute-start | bytes 49160 | tf_op jit(solution)/shard_map/ppermute | solution.py:14
  145.4 4.7 %collective-permute-start.21 = (f32[2,1,16,128]{3,2,1,0:T(8,128)S(1)}, f32[2,1,16,128]{3,2,1,0:T(8,128)S(1)}, u32[]{:S(2)}, u32[]{:S(2)}) collective-permute-start(f32[2,1,16,128]{3,2,1,0:T(8,128)S(1)} %slice.1473), channel_id=1, source_target_pairs={{2,0},{4,2},{6,4},{8,6},{10,8},{12,10},{14,12},{3,1},{5,3},{7,5},{... | collective-permute-start | bytes 49160 | tf_op jit(solution)/shard_map/ppermute | solution.py:14
  151.7 9.8 %collective-permute-start.22 = (f32[2,16,1,128]{3,1,2,0:T(8,128)S(1)}, f32[2,16,1,128]{3,1,2,0:T(8,128)S(1)}, u32[]{:S(2)}, u32[]{:S(2)}) collective-permute-start(f32[2,16,1,128]{3,1,2,0:T(8,128)S(1)} %bitcast.597), channel_id=1, source_target_pairs={{0,1},{2,3},{4,5},{6,7},{8,9},{10,11},{12,13},{14,15},{16,17},{18,... | collective-permute-start | bytes 49160 | tf_op jit(solution)/shard_map/ppermute | solution.py:14
  157.8 4.5 %collective-permute-start.23 = (f32[2,1,16,128]{3,2,1,0:T(8,128)S(1)}, f32[2,1,16,128]{3,2,1,0:T(8,128)S(1)}, u32[]{:S(2)}, u32[]{:S(2)}) collective-permute-start(f32[2,1,16,128]{3,2,1,0:T(8,128)S(1)} %slice.1486), channel_id=1, source_target_pairs={{0,2},{2,4},{4,6},{6,8},{8,10},{10,12},{12,14},{1,3},{3,5},{5,7},{... | collective-permute-start | bytes 49160 | tf_op jit(solution)/shard_map/ppermute | solution.py:14
  169.3 6.0 %collective-permute-start.24 = (f32[2,16,1,128]{3,1,2,0:T(8,128)S(1)}, f32[2,16,1,128]{3,1,2,0:T(8,128)S(1)}, u32[]{:S(2)}, u32[]{:S(2)}) collective-permute-start(f32[2,16,1,128]{3,1,2,0:T(8,128)S(1)} %bitcast.591), channel_id=1, source_target_pairs={{1,0},{3,2},{5,4},{7,6},{9,8},{11,10},{13,12},{15,14},{17,16},{19,... | collective-permute-start | bytes 49160 | tf_op jit(solution)/shard_map/ppermute | solution.py:14
  170.7 5.0 %collective-permute-start.25 = (f32[2,1,16,128]{3,2,1,0:T(8,128)S(1)}, f32[2,1,16,128]{3,2,1,0:T(8,128)S(1)}, u32[]{:S(2)}, u32[]{:S(2)}) collective-permute-start(f32[2,1,16,128]{3,2,1,0:T(8,128)S(1)} %slice.1504), channel_id=1, source_target_pairs={{2,0},{4,2},{6,4},{8,6},{10,8},{12,10},{14,12},{3,1},{5,3},{7,5},{... | collective-permute-start | bytes 49160 | tf_op jit(solution)/shard_map/ppermute | solution.py:14
  177.5 9.8 %collective-permute-start.26 = (f32[2,16,1,128]{3,1,2,0:T(8,128)S(1)}, f32[2,16,1,128]{3,1,2,0:T(8,128)S(1)}, u32[]{:S(2)}, u32[]{:S(2)}) collective-permute-start(f32[2,16,1,128]{3,1,2,0:T(8,128)S(1)} %bitcast.598), channel_id=1, source_target_pairs={{0,1},{2,3},{4,5},{6,7},{8,9},{10,11},{12,13},{14,15},{16,17},{18,... | collective-permute-start | bytes 49160 | tf_op jit(solution)/shard_map/ppermute | solution.py:14
  183.6 4.5 %collective-permute-start.27 = (f32[2,1,16,128]{3,2,1,0:T(8,128)S(1)}, f32[2,1,16,128]{3,2,1,0:T(8,128)S(1)}, u32[]{:S(2)}, u32[]{:S(2)}) collective-permute-start(f32[2,1,16,128]{3,2,1,0:T(8,128)S(1)} %slice.1517), channel_id=1, source_target_pairs={{0,2},{2,4},{4,6},{6,8},{8,10},{10,12},{12,14},{1,3},{3,5},{5,7},{... | collective-permute-start | bytes 49160 | tf_op jit(solution)/shard_map/ppermute | solution.py:14
  195.3 6.0 %collective-permute-start.28 = (f32[2,16,1,128]{3,2,1,0:T(1,128)S(1)}, f32[2,16,1,128]{3,2,1,0:T(1,128)S(1)}, u32[]{:S(2)}, u32[]{:S(2)}) collective-permute-start(f32[2,16,1,128]{3,2,1,0:T(1,128)S(1)} %slice.1285), channel_id=1, source_target_pairs={{1,0},{3,2},{5,4},{7,6},{9,8},{11,10},{13,12},{15,14},{17,16},{19,... | collective-permute-start | bytes 49160 | tf_op jit(solution)/shard_map/ppermute | solution.py:14
  196.7 4.7 %collective-permute-start.29 = (f32[2,1,16,128]{3,2,1,0:T(8,128)S(1)}, f32[2,1,16,128]{3,2,1,0:T(8,128)S(1)}, u32[]{:S(2)}, u32[]{:S(2)}) collective-permute-start(f32[2,1,16,128]{3,2,1,0:T(8,128)S(1)} %slice.1535), channel_id=1, source_target_pairs={{2,0},{4,2},{6,4},{8,6},{10,8},{12,10},{14,12},{3,1},{5,3},{7,5},{... | collective-permute-start | bytes 49160 | tf_op jit(solution)/shard_map/ppermute | solution.py:14
  203.1 9.8 %collective-permute-start.30 = (f32[2,16,1,128]{3,1,2,0:T(8,128)S(1)}, f32[2,16,1,128]{3,1,2,0:T(8,128)S(1)}, u32[]{:S(2)}, u32[]{:S(2)}) collective-permute-start(f32[2,16,1,128]{3,1,2,0:T(8,128)S(1)} %bitcast.599), channel_id=1, source_target_pairs={{0,1},{2,3},{4,5},{6,7},{8,9},{10,11},{12,13},{14,15},{16,17},{18,... | collective-permute-start | bytes 49160 | tf_op jit(solution)/shard_map/ppermute | solution.py:14
  (83 other events, 121.2 us)
Sparse Core Ops, SparseCore 0:
  217.1 75.4 reduce-scatter.1
where the time goes:
time: 329 us; the launch traced here: 327 us
  blocking collectives  100 us (30%)
  starting transfers between devices  99.3 us (30%)
  local copies, waits for them, and re-layouts  54.1 us (16%)
  waiting for transfers between devices  27.5 us (8%)
  between operations  19.4 us (6%)
  other arithmetic  18.6 us (6%)
  matrix products  7.47 us (2%)
    psum x1, blocking collectives, on_device(): misfit = lax.psum(local_misfit, ('tx', 'gx', 'gy'))  100 us
    ppermute x32, starting transfers between devices, shifted(): return lax.ppermute(x, axis, pairs)  99.2 us
    ppermute x32, waiting for transfers between devices, shifted(): return lax.ppermute(x, axis, pairs)  27.5 us
    unnamed x167, local copies, waits for them, and re-layouts  21.2 us
    scatter-add x4, local copies, waits for them, and re-layouts, on_device(): adj_e.at[0:2, :, :, ZREC]  14.4 us
    another operation x6, other arithmetic  10.1 us
  transfers between devices with their start and end apart: 33, of which 20 were waited for; matrix products, arithmetic and copies ran while one was open for 4% of the time, Pallas kernels for 0%

commit v1 on v0

--- a/solution.py
+++ b/solution.py
@@ -119,7 +119,7 @@
     local_misfit = jnp.float32(0.0)
     for step_idx in range(STEPS):
         local_misfit = local_misfit + 0.5 * jnp.sum(residuals[step_idx] * residuals[step_idx])
-    misfit = lax.psum(local_misfit, ("tx", "gx", "gy"))
+    misfit = lax.psum(lax.psum(local_misfit, "tx"), ("gx", "gy"))
     tile_flag = footprint[0, 0, 0].astype(jnp.float32)
     gradient = jnp.stack([grad_h, grad_v]) * tile_flag
     groups_count = lax.axis_size("tx")

time: 329 us -> 314 us (0.954)
  the two profiles are of different devices: /device:TPU:1 before, /device:TPU:16 now
where the time goes in v1:
time: 314 us; the launch traced here: 312 us
  starting transfers between devices  102 us (32%)
  blocking collectives  67.3 us (21%)
  local copies, waits for them, and re-layouts  56 us (18%)
  waiting for transfers between devices  40.3 us (13%)
  other arithmetic  19.8 us (6%)
  between operations  19.3 us (6%)
  matrix products  7.44 us (2%)
    ppermute x32, starting transfers between devices, shifted(): return lax.ppermute(x, axis, pairs)  102 us
    psum x2, blocking collectives, on_device(): misfit = lax.psum(lax.psum(local_misfit, 'tx'), ('gx', 'gy'))  67.3 us
    ppermute x32, waiting for transfers between devices, shifted(): return lax.ppermute(x, axis, pairs)  40.2 us
    unnamed x167, local copies, waits for them, and re-layouts  21.2 us
    scatter-add x4, local copies, waits for them, and re-layouts, on_device(): adj_e.at[0:2, :, :, ZREC]  16.3 us
    another operation x6, other arithmetic  11.3 us
  transfers between devices with their start and end apart: 33, of which 23 were waited for; matrix products, arithmetic and copies ran while one was open for 4% of the time, Pallas kernels for 0%

profile of v1, /device:TPU:16, one launch (start us, length us, event | category | flops | bytes accessed | tf_op | source)
XLA Modules:
  0.0 312.1 jit_solution(15283104082053208149)
XLA Ops:
  8.3 4.0 %collective-permute-start = (f32[2,16,1,128]{3,2,1,0:T(1,128)S(1)}, f32[2,16,1,128]{3,2,1,0:T(1,128)S(1)}, u32[]{:S(2)}, u32[]{:S(2)}) collective-permute-start(f32[2,16,1,128]{3,2,1,0:T(1,128)S(1)} %slice.1044), channel_id=1, source_target_pairs={{1,0},{3,2},{5,4},{7,6},{9,8},{11,10},{13,12},{15,14},{17,16},{19,... | collective-permute-start | bytes 49160 | tf_op jit(solution)/shard_map/ppermute | solution.py:14
  23.2 4.5 %collective-permute-start.3 = (f32[2,1,16,128]{3,2,1,0:T(8,128)S(1)}, f32[2,1,16,128]{3,2,1,0:T(8,128)S(1)}, u32[]{:S(2)}, u32[]{:S(2)}) collective-permute-start(f32[2,1,16,128]{3,2,1,0:T(8,128)S(1)} %slice.1340), channel_id=1, source_target_pairs={{0,2},{2,4},{4,6},{6,8},{8,10},{10,12},{12,14},{1,3},{3,5},{5,7},{... | collective-permute-start | bytes 49160 | tf_op jit(solution)/shard_map/ppermute | solution.py:14
  31.4 5.4 %collective-permute-start.4 = (f32[2,16,1,128]{3,2,1,0:T(1,128)S(1)}, f32[2,16,1,128]{3,2,1,0:T(1,128)S(1)}, u32[]{:S(2)}, u32[]{:S(2)}) collective-permute-start(f32[2,16,1,128]{3,2,1,0:T(1,128)S(1)} %slice.1076), channel_id=1, source_target_pairs={{1,0},{3,2},{5,4},{7,6},{9,8},{11,10},{13,12},{15,14},{17,16},{19,... | collective-permute-start | bytes 49160 | tf_op jit(solution)/shard_map/ppermute | solution.py:14
  46.6 4.8 %collective-permute-start.7 = (f32[2,1,16,128]{3,2,1,0:T(8,128)S(1)}, f32[2,1,16,128]{3,2,1,0:T(8,128)S(1)}, u32[]{:S(2)}, u32[]{:S(2)}) collective-permute-start(f32[2,1,16,128]{3,2,1,0:T(8,128)S(1)} %slice.1368), channel_id=1, source_target_pairs={{0,2},{2,4},{4,6},{6,8},{8,10},{10,12},{12,14},{1,3},{3,5},{5,7},{... | collective-permute-start | bytes 49160 | tf_op jit(solution)/shard_map/ppermute | solution.py:14
  58.3 5.4 %collective-permute-start.8 = (f32[2,16,1,128]{3,2,1,0:T(1,128)S(1)}, f32[2,16,1,128]{3,2,1,0:T(1,128)S(1)}, u32[]{:S(2)}, u32[]{:S(2)}) collective-permute-start(f32[2,16,1,128]{3,2,1,0:T(1,128)S(1)} %copy-done.74), channel_id=1, source_target_pairs={{1,0},{3,2},{5,4},{7,6},{9,8},{11,10},{13,12},{15,14},{17,16},{19,... | collective-permute-start | bytes 49160 | tf_op jit(solution)/shard_map/ppermute | solution.py:14
  66.2 4.1 %collective-permute-done.9 = f32[2,1,16,128]{3,2,1,0:T(8,128)S(1)} collective-permute-done((f32[2,1,16,128]{3,2,1,0:T(8,128)S(1)}, f32[2,1,16,128]{3,2,1,0:T(8,128)S(1)}, u32[]{:S(2)}, u32[]{:S(2)}) %collective-permute-start.9) | collective-permute-done | bytes 16416 | tf_op jit(solution)/shard_map/ppermute | solution.py:14
  74.9 4.8 %collective-permute-start.11 = (f32[2,1,16,128]{3,2,1,0:T(8,128)S(1)}, f32[2,1,16,128]{3,2,1,0:T(8,128)S(1)}, u32[]{:S(2)}, u32[]{:S(2)}) collective-permute-start(f32[2,1,16,128]{3,2,1,0:T(8,128)S(1)} %slice.1396), channel_id=1, source_target_pairs={{0,2},{2,4},{4,6},{6,8},{8,10},{10,12},{12,14},{1,3},{3,5},{5,7},{... | collective-permute-start | bytes 49160 | tf_op jit(solution)/shard_map/ppermute | solution.py:14
  88.3 6.2 %collective-permute-start.12 = (f32[2,16,1,128]{3,1,2,0:T(8,128)}, f32[2,16,1,128]{3,1,2,0:T(8,128)}, u32[]{:S(2)}, u32[]{:S(2)}) collective-permute-start(f32[2,16,1,128]{3,1,2,0:T(8,128)} %bitcast.197), channel_id=1, source_target_pairs={{1,0},{3,2},{5,4},{7,6},{9,8},{11,10},{13,12},{15,14},{17,16},{19,... | collective-permute-start | bytes 49160 | tf_op jit(solution)/shard_map/ppermute | solution.py:14
  98.8 2.3 collective-permute-done.13
  106.6 4.8 %collective-permute-start.15 = (f32[2,1,16,128]{3,2,1,0:T(8,128)S(1)}, f32[2,1,16,128]{3,2,1,0:T(8,128)S(1)}, u32[]{:S(2)}, u32[]{:S(2)}) collective-permute-start(f32[2,1,16,128]{3,2,1,0:T(8,128)S(1)} %slice.1424), channel_id=1, source_target_pairs={{0,2},{2,4},{4,6},{6,8},{8,10},{10,12},{12,14},{1,3},{3,5},{5,7},{... | collective-permute-start | bytes 49160 | tf_op jit(solution)/shard_map/ppermute | solution.py:14
  117.3 2.0 add_select_fusion.3
  119.3 3.6 %scatter-add.14 = f32[3,16,16,128]{3,2,1,0:T(8,128)S(1)} dynamic-update-slice(f32[3,16,16,128]{3,2,1,0:T(8,128)S(1)} %get-tuple-element.51, f32[2,16,16,1]{3,2,1,0:T(8,128)S(1)} %add_select_fusion.3, s32[]{:T(128)} %bitcast.4, s32[]{:T(128)} %constant.106.clone.1, s32[]{:T(128)} %constant.106.clone.1, s32[]{:T(128)} %bitcast.5) | dynamic-update-slice | bytes 4100 | tf_op jit(solution)/shard_map/scatter-add | solution.py:112
  123.0 5.4 %collective-permute-start.16 = (f32[2,16,1,128]{3,1,2,0:T(8,128)S(1)}, f32[2,16,1,128]{3,1,2,0:T(8,128)S(1)}, u32[]{:S(2)}, u32[]{:S(2)}) collective-permute-start(f32[2,16,1,128]{3,1,2,0:T(8,128)S(1)} %bitcast.589), channel_id=1, source_target_pairs={{1,0},{3,2},{5,4},{7,6},{9,8},{11,10},{13,12},{15,14},{17,16},{19,... | collective-permute-start | bytes 49160 | tf_op jit(solution)/shard_map/ppermute | solution.py:14
  129.9 5.2 %collective-permute-done.17 = f32[2,1,16,128]{3,2,1,0:T(8,128)S(1)} collective-permute-done((f32[2,1,16,128]{3,2,1,0:T(8,128)S(1)}, f32[2,1,16,128]{3,2,1,0:T(8,128)S(1)}, u32[]{:S(2)}, u32[]{:S(2)}) %collective-permute-start.17) | collective-permute-done | bytes 16416 | tf_op jit(solution)/shard_map/ppermute | solution.py:14
  137.8 4.8 %collective-permute-start.19 = (f32[2,1,16,128]{3,2,1,0:T(8,128)S(1)}, f32[2,1,16,128]{3,2,1,0:T(8,128)S(1)}, u32[]{:S(2)}, u32[]{:S(2)}) collective-permute-start(f32[2,1,16,128]{3,2,1,0:T(8,128)S(1)} %slice.1453), channel_id=1, source_target_pairs={{0,2},{2,4},{4,6},{6,8},{8,10},{10,12},{12,14},{1,3},{3,5},{5,7},{... | collective-permute-start | bytes 49160 | tf_op jit(solution)/shard_map/ppermute | solution.py:14
  145.3 2.0 add_select_fusion.2
  147.3 3.6 %scatter-add.15 = f32[3,16,16,128]{3,2,1,0:T(8,128)S(1)} dynamic-update-slice(f32[3,16,16,128]{3,2,1,0:T(8,128)S(1)} %copy.87, f32[2,16,16,1]{3,2,1,0:T(8,128)S(1)} %add_select_fusion.2, s32[]{:T(128)} %bitcast.4, s32[]{:T(128)} %constant.106.clone.1, s32[]{:T(128)} %constant.106.clone.1, s32[]{:T(128)} %bitcast.5) | dynamic-update-slice | bytes 4100 | tf_op jit(solution)/shard_map/scatter-add | solution.py:112
  151.0 5.4 %collective-permute-start.20 = (f32[2,16,1,128]{3,1,2,0:T(8,128)S(1)}, f32[2,16,1,128]{3,1,2,0:T(8,128)S(1)}, u32[]{:S(2)}, u32[]{:S(2)}) collective-permute-start(f32[2,16,1,128]{3,1,2,0:T(8,128)S(1)} %bitcast.590), channel_id=1, source_target_pairs={{1,0},{3,2},{5,4},{7,6},{9,8},{11,10},{13,12},{15,14},{17,16},{19,... | collective-permute-start | bytes 49160 | tf_op jit(solution)/shard_map/ppermute | solution.py:14
  157.9 5.2 %collective-permute-done.21 = f32[2,1,16,128]{3,2,1,0:T(8,128)S(1)} collective-permute-done((f32[2,1,16,128]{3,2,1,0:T(8,128)S(1)}, f32[2,1,16,128]{3,2,1,0:T(8,128)S(1)}, u32[]{:S(2)}, u32[]{:S(2)}) %collective-permute-start.21) | collective-permute-done | bytes 16416 | tf_op jit(solution)/shard_map/ppermute | solution.py:14
  166.0 4.8 %collective-permute-start.23 = (f32[2,1,16,128]{3,2,1,0:T(8,128)S(1)}, f32[2,1,16,128]{3,2,1,0:T(8,128)S(1)}, u32[]{:S(2)}, u32[]{:S(2)}) collective-permute-start(f32[2,1,16,128]{3,2,1,0:T(8,128)S(1)} %slice.1486), channel_id=1, source_target_pairs={{0,2},{2,4},{4,6},{6,8},{8,10},{10,12},{12,14},{1,3},{3,5},{5,7},{... | collective-permute-start | bytes 49160 | tf_op jit(solution)/shard_map/ppermute | solution.py:14
  173.5 2.7 add_select_fusion.1
  176.2 4.5 %scatter-add.16 = f32[3,16,16,128]{3,2,1,0:T(8,128)S(1)} dynamic-update-slice(f32[3,16,16,128]{3,2,1,0:T(8,128)S(1)} %copy.88, f32[2,16,16,1]{3,2,1,0:T(8,128)} %add_select_fusion.1, s32[]{:T(128)} %bitcast.4, s32[]{:T(128)} %constant.106.clone.1, s32[]{:T(128)} %constant.106.clone.1, s32[]{:T(128)} %bitcast.5) | dynamic-update-slice | bytes 4100 | tf_op jit(solution)/shard_map/scatter-add | solution.py:112
  180.8 5.4 %collective-permute-start.24 = (f32[2,16,1,128]{3,1,2,0:T(8,128)S(1)}, f32[2,16,1,128]{3,1,2,0:T(8,128)S(1)}, u32[]{:S(2)}, u32[]{:S(2)}) collective-permute-start(f32[2,16,1,128]{3,1,2,0:T(8,128)S(1)} %bitcast.591), channel_id=1, source_target_pairs={{1,0},{3,2},{5,4},{7,6},{9,8},{11,10},{13,12},{15,14},{17,16},{19,... | collective-permute-start | bytes 49160 | tf_op jit(solution)/shard_map/ppermute | solution.py:14
  187.9 5.0 %collective-permute-done.25 = f32[2,1,16,128]{3,2,1,0:T(8,128)S(1)} collective-permute-done((f32[2,1,16,128]{3,2,1,0:T(8,128)S(1)}, f32[2,1,16,128]{3,2,1,0:T(8,128)S(1)}, u32[]{:S(2)}, u32[]{:S(2)}) %collective-permute-start.25) | collective-permute-done | bytes 16416 | tf_op jit(solution)/shard_map/ppermute | solution.py:14
  195.9 4.8 %collective-permute-start.27 = (f32[2,1,16,128]{3,2,1,0:T(8,128)S(1)}, f32[2,1,16,128]{3,2,1,0:T(8,128)S(1)}, u32[]{:S(2)}, u32[]{:S(2)}) collective-permute-start(f32[2,1,16,128]{3,2,1,0:T(8,128)S(1)} %slice.1517), channel_id=1, source_target_pairs={{0,2},{2,4},{4,6},{6,8},{8,10},{10,12},{12,14},{1,3},{3,5},{5,7},{... | collective-permute-start | bytes 49160 | tf_op jit(solution)/shard_map/ppermute | solution.py:14
  203.6 2.7 add_select_fusion
  206.3 4.5 %scatter-add.19 = f32[3,16,16,128]{3,2,1,0:T(8,128)S(1)} dynamic-update-slice(f32[3,16,16,128]{3,2,1,0:T(8,128)S(1)} %copy.89, f32[2,16,16,1]{3,2,1,0:T(8,128)} %add_select_fusion, s32[]{:T(128)} %bitcast.4, s32[]{:T(128)} %constant.106.clone.1, s32[]{:T(128)} %constant.106.clone.1, s32[]{:T(128)} %bitcast.5) | dynamic-update-slice | bytes 4100 | tf_op jit(solution)/shard_map/scatter-add | solution.py:112
  210.9 5.4 %collective-permute-start.28 = (f32[2,16,1,128]{3,2,1,0:T(1,128)S(1)}, f32[2,16,1,128]{3,2,1,0:T(1,128)S(1)}, u32[]{:S(2)}, u32[]{:S(2)}) collective-permute-start(f32[2,16,1,128]{3,2,1,0:T(1,128)S(1)} %slice.1285), channel_id=1, source_target_pairs={{1,0},{3,2},{5,4},{7,6},{9,8},{11,10},{13,12},{15,14},{17,16},{19,... | collective-permute-start | bytes 49160 | tf_op jit(solution)/shard_map/ppermute | solution.py:14
  217.8 5.2 %collective-permute-done.29 = f32[2,1,16,128]{3,2,1,0:T(8,128)S(1)} collective-permute-done((f32[2,1,16,128]{3,2,1,0:T(8,128)S(1)}, f32[2,1,16,128]{3,2,1,0:T(8,128)S(1)}, u32[]{:S(2)}, u32[]{:S(2)}) %collective-permute-start.29) | collective-permute-done | bytes 16416 | tf_op jit(solution)/shard_map/ppermute | solution.py:14
  226.1 4.8 %collective-permute-start.31 = (f32[2,1,16,128]{3,2,1,0:T(8,128)S(1)}, f32[2,1,16,128]{3,2,1,0:T(8,128)S(1)}, u32[]{:S(2)}, u32[]{:S(2)}) collective-permute-start(f32[2,1,16,128]{3,2,1,0:T(8,128)S(1)} %slice.1548), channel_id=1, source_target_pairs={{0,2},{2,4},{4,6},{6,8},{8,10},{10,12},{12,14},{1,3},{3,5},{5,7},{... | collective-permute-start | bytes 49160 | tf_op jit(solution)/shard_map/ppermute | solution.py:14
  237.9 26.3 %psum.14 = f32[]{:T(128)} all-reduce(f32[]{:T(128)S(6)} %add.231), channel_id=1, replica_groups=mesh['tx'=16,'gx'=8,'gy'=2] {'tx'}, use_global_device_ids=true, to_apply=%region_6.0 | all-reduce | flops 1 | bytes 8 | tf_op jit(solution)/shard_map/psum | solution.py:122
  264.2 41.1 %psum.15 = f32[]{:T(128)} all-reduce(f32[]{:T(128)} %psum.14), channel_id=1, replica_groups=mesh['tx'=16,'gx'=8,'gy'=2] {'gx','gy'}, use_global_device_ids=true, to_apply=%region_7.0 | all-reduce | flops 1 | bytes 8 | tf_op jit(solution)/shard_map/psum | solution.py:122
  (430 shorter events, 91.8 us)
Async XLA Ops:
  7.2 298.1 %reduce-scatter.2.cloned.1.call-start = ((), (), s32[]{:S(2)}) async-start(), calls=%async_computation.1 | async-start | bytes 278528 | tf_op jit(solution)/shard_map/reduce_scatter | solution.py:129
  8.3 13.2 %collective-permute-start = (f32[2,16,1,128]{3,2,1,0:T(1,128)S(1)}, f32[2,16,1,128]{3,2,1,0:T(1,128)S(1)}, u32[]{:S(2)}, u32[]{:S(2)}) collective-permute-start(f32[2,16,1,128]{3,2,1,0:T(1,128)S(1)} %slice.1044), channel_id=1, source_target_pairs={{1,0},{3,2},{5,4},{7,6},{9,8},{11,10},{13,12},{15,14},{17,16},{19,... | collective-permute-start | bytes 49160 | tf_op jit(solution)/shard_map/ppermute | solution.py:14
  12.3 9.2 %collective-permute-start.1 = (f32[2,1,16,128]{3,2,1,0:T(8,128)S(1)}, f32[2,1,16,128]{3,2,1,0:T(8,128)S(1)}, u32[]{:S(2)}, u32[]{:S(2)}) collective-permute-start(f32[2,1,16,128]{3,2,1,0:T(8,128)S(1)} %slice.1328), channel_id=1, source_target_pairs={{2,0},{4,2},{6,4},{8,6},{10,8},{12,10},{14,12},{3,1},{5,3},{7,5},{... | collective-permute-start | bytes 49160 | tf_op jit(solution)/shard_map/ppermute | solution.py:14
  21.8 7.1 %collective-permute-start.2 = (f32[2,16,1,128]{3,1,2,0:T(8,128)S(1)}, f32[2,16,1,128]{3,1,2,0:T(8,128)S(1)}, u32[]{:S(2)}, u32[]{:S(2)}) collective-permute-start(f32[2,16,1,128]{3,1,2,0:T(8,128)S(1)} %bitcast.592), channel_id=1, source_target_pairs={{0,1},{2,3},{4,5},{6,7},{8,9},{10,11},{12,13},{14,15},{16,17},{18,... | collective-permute-start | bytes 49160 | tf_op jit(solution)/shard_map/ppermute | solution.py:14
  31.4 10.1 %collective-permute-start.4 = (f32[2,16,1,128]{3,2,1,0:T(1,128)S(1)}, f32[2,16,1,128]{3,2,1,0:T(1,128)S(1)}, u32[]{:S(2)}, u32[]{:S(2)}) collective-permute-start(f32[2,16,1,128]{3,2,1,0:T(1,128)S(1)} %slice.1076), channel_id=1, source_target_pairs={{1,0},{3,2},{5,4},{7,6},{9,8},{11,10},{13,12},{15,14},{17,16},{19,... | collective-permute-start | bytes 49160 | tf_op jit(solution)/shard_map/ppermute | solution.py:14
  36.8 6.5 %collective-permute-start.5 = (f32[2,1,16,128]{3,2,1,0:T(8,128)S(1)}, f32[2,1,16,128]{3,2,1,0:T(8,128)S(1)}, u32[]{:S(2)}, u32[]{:S(2)}) collective-permute-start(f32[2,1,16,128]{3,2,1,0:T(8,128)S(1)} %slice.1355), channel_id=1, source_target_pairs={{2,0},{4,2},{6,4},{8,6},{10,8},{12,10},{14,12},{3,1},{5,3},{7,5},{... | collective-permute-start | bytes 49160 | tf_op jit(solution)/shard_map/ppermute | solution.py:14
  45.2 7.1 %collective-permute-start.6 = (f32[2,16,1,128]{3,1,2,0:T(8,128)S(1)}, f32[2,16,1,128]{3,1,2,0:T(8,128)S(1)}, u32[]{:S(2)}, u32[]{:S(2)}) collective-permute-start(f32[2,16,1,128]{3,1,2,0:T(8,128)S(1)} %bitcast.593), channel_id=1, source_target_pairs={{0,1},{2,3},{4,5},{6,7},{8,9},{10,11},{12,13},{14,15},{16,17},{18,... | collective-permute-start | bytes 49160 | tf_op jit(solution)/shard_map/ppermute | solution.py:14
  46.6 6.3 %collective-permute-start.7 = (f32[2,1,16,128]{3,2,1,0:T(8,128)S(1)}, f32[2,1,16,128]{3,2,1,0:T(8,128)S(1)}, u32[]{:S(2)}, u32[]{:S(2)}) collective-permute-start(f32[2,1,16,128]{3,2,1,0:T(8,128)S(1)} %slice.1368), channel_id=1, source_target_pairs={{0,2},{2,4},{4,6},{6,8},{8,10},{10,12},{12,14},{1,3},{3,5},{5,7},{... | collective-permute-start | bytes 49160 | tf_op jit(solution)/shard_map/ppermute | solution.py:14
  58.3 7.9 %collective-permute-start.8 = (f32[2,16,1,128]{3,2,1,0:T(1,128)S(1)}, f32[2,16,1,128]{3,2,1,0:T(1,128)S(1)}, u32[]{:S(2)}, u32[]{:S(2)}) collective-permute-start(f32[2,16,1,128]{3,2,1,0:T(1,128)S(1)} %copy-done.74), channel_id=1, source_target_pairs={{1,0},{3,2},{5,4},{7,6},{9,8},{11,10},{13,12},{15,14},{17,16},{19,... | collective-permute-start | bytes 49160 | tf_op jit(solution)/shard_map/ppermute | solution.py:14
  63.8 6.5 %collective-permute-start.9 = (f32[2,1,16,128]{3,2,1,0:T(8,128)S(1)}, f32[2,1,16,128]{3,2,1,0:T(8,128)S(1)}, u32[]{:S(2)}, u32[]{:S(2)}) collective-permute-start(f32[2,1,16,128]{3,2,1,0:T(8,128)S(1)} %copy-done.72), channel_id=1, source_target_pairs={{2,0},{4,2},{6,4},{8,6},{10,8},{12,10},{14,12},{3,1},{5,3},{7,5},{... | collective-permute-start | bytes 49160 | tf_op jit(solution)/shard_map/ppermute | solution.py:14
  73.6 7.1 %collective-permute-start.10 = (f32[2,16,1,128]{3,1,2,0:T(8,128)S(1)}, f32[2,16,1,128]{3,1,2,0:T(8,128)S(1)}, u32[]{:S(2)}, u32[]{:S(2)}) collective-permute-start(f32[2,16,1,128]{3,1,2,0:T(8,128)S(1)} %bitcast.594), channel_id=1, source_target_pairs={{0,1},{2,3},{4,5},{6,7},{8,9},{10,11},{12,13},{14,15},{16,17},{18,... | collective-permute-start | bytes 49160 | tf_op jit(solution)/shard_map/ppermute | solution.py:14
  74.9 6.3 %collective-permute-start.11 = (f32[2,1,16,128]{3,2,1,0:T(8,128)S(1)}, f32[2,1,16,128]{3,2,1,0:T(8,128)S(1)}, u32[]{:S(2)}, u32[]{:S(2)}) collective-permute-start(f32[2,1,16,128]{3,2,1,0:T(8,128)S(1)} %slice.1396), channel_id=1, source_target_pairs={{0,2},{2,4},{4,6},{6,8},{8,10},{10,12},{12,14},{1,3},{3,5},{5,7},{... | collective-permute-start | bytes 49160 | tf_op jit(solution)/shard_map/ppermute | solution.py:14
  88.3 9.8 %collective-permute-start.12 = (f32[2,16,1,128]{3,1,2,0:T(8,128)}, f32[2,16,1,128]{3,1,2,0:T(8,128)}, u32[]{:S(2)}, u32[]{:S(2)}) collective-permute-start(f32[2,16,1,128]{3,1,2,0:T(8,128)} %bitcast.197), channel_id=1, source_target_pairs={{1,0},{3,2},{5,4},{7,6},{9,8},{11,10},{13,12},{15,14},{17,16},{19,... | collective-permute-start | bytes 49160 | tf_op jit(solution)/shard_map/ppermute | solution.py:14
  94.5 6.6 %collective-permute-start.13 = (f32[2,1,16,128]{3,2,1,0:T(8,128)S(1)}, f32[2,1,16,128]{3,2,1,0:T(8,128)}, u32[]{:S(2)}, u32[]{:S(2)}) collective-permute-start(f32[2,1,16,128]{3,2,1,0:T(8,128)S(1)} %copy-done.73), channel_id=1, source_target_pairs={{2,0},{4,2},{6,4},{8,6},{10,8},{12,10},{14,12},{3,1},{5,3},{7,5},{... | collective-permute-start | bytes 49160 | tf_op jit(solution)/shard_map/ppermute | solution.py:14
  105.3 7.1 %collective-permute-start.14 = (f32[2,16,1,128]{3,1,2,0:T(8,128)S(1)}, f32[2,16,1,128]{3,1,2,0:T(8,128)S(1)}, u32[]{:S(2)}, u32[]{:S(2)}) collective-permute-start(f32[2,16,1,128]{3,1,2,0:T(8,128)S(1)} %bitcast.595), channel_id=1, source_target_pairs={{0,1},{2,3},{4,5},{6,7},{8,9},{10,11},{12,13},{14,15},{16,17},{18,... | collective-permute-start | bytes 49160 | tf_op jit(solution)/shard_map/ppermute | solution.py:14
  106.6 6.3 %collective-permute-start.15 = (f32[2,1,16,128]{3,2,1,0:T(8,128)S(1)}, f32[2,1,16,128]{3,2,1,0:T(8,128)S(1)}, u32[]{:S(2)}, u32[]{:S(2)}) collective-permute-start(f32[2,1,16,128]{3,2,1,0:T(8,128)S(1)} %slice.1424), channel_id=1, source_target_pairs={{0,2},{2,4},{4,6},{6,8},{8,10},{10,12},{12,14},{1,3},{3,5},{5,7},{... | collective-permute-start | bytes 49160 | tf_op jit(solution)/shard_map/ppermute | solution.py:14
  123.0 6.9 %collective-permute-start.16 = (f32[2,16,1,128]{3,1,2,0:T(8,128)S(1)}, f32[2,16,1,128]{3,1,2,0:T(8,128)S(1)}, u32[]{:S(2)}, u32[]{:S(2)}) collective-permute-start(f32[2,16,1,128]{3,1,2,0:T(8,128)S(1)} %bitcast.589), channel_id=1, source_target_pairs={{1,0},{3,2},{5,4},{7,6},{9,8},{11,10},{13,12},{15,14},{17,16},{19,... | collective-permute-start | bytes 49160 | tf_op jit(solution)/shard_map/ppermute | solution.py:14
  128.5 6.5 %collective-permute-start.17 = (f32[2,1,16,128]{3,2,1,0:T(8,128)S(1)}, f32[2,1,16,128]{3,2,1,0:T(8,128)S(1)}, u32[]{:S(2)}, u32[]{:S(2)}) collective-permute-start(f32[2,1,16,128]{3,2,1,0:T(8,128)S(1)} %slice.1440), channel_id=1, source_target_pairs={{2,0},{4,2},{6,4},{8,6},{10,8},{12,10},{14,12},{3,1},{5,3},{7,5},{... | collective-permute-start | bytes 49160 | tf_op jit(solution)/shard_map/ppermute | solution.py:14
  136.4 7.1 %collective-permute-start.18 = (f32[2,16,1,128]{3,1,2,0:T(8,128)S(1)}, f32[2,16,1,128]{3,1,2,0:T(8,128)S(1)}, u32[]{:S(2)}, u32[]{:S(2)}) collective-permute-start(f32[2,16,1,128]{3,1,2,0:T(8,128)S(1)} %bitcast.596), channel_id=1, source_target_pairs={{0,1},{2,3},{4,5},{6,7},{8,9},{10,11},{12,13},{14,15},{16,17},{18,... | collective-permute-start | bytes 49160 | tf_op jit(solution)/shard_map/ppermute | solution.py:14
  137.8 6.3 %collective-permute-start.19 = (f32[2,1,16,128]{3,2,1,0:T(8,128)S(1)}, f32[2,1,16,128]{3,2,1,0:T(8,128)S(1)}, u32[]{:S(2)}, u32[]{:S(2)}) collective-permute-start(f32[2,1,16,128]{3,2,1,0:T(8,128)S(1)} %slice.1453), channel_id=1, source_target_pairs={{0,2},{2,4},{4,6},{6,8},{8,10},{10,12},{12,14},{1,3},{3,5},{5,7},{... | collective-permute-start | bytes 49160 | tf_op jit(solution)/shard_map/ppermute | solution.py:14
  151.0 6.9 %collective-permute-start.20 = (f32[2,16,1,128]{3,1,2,0:T(8,128)S(1)}, f32[2,16,1,128]{3,1,2,0:T(8,128)S(1)}, u32[]{:S(2)}, u32[]{:S(2)}) collective-permute-start(f32[2,16,1,128]{3,1,2,0:T(8,128)S(1)} %bitcast.590), channel_id=1, source_target_pairs={{1,0},{3,2},{5,4},{7,6},{9,8},{11,10},{13,12},{15,14},{17,16},{19,... | collective-permute-start | bytes 49160 | tf_op jit(solution)/shard_map/ppermute | solution.py:14
  156.6 6.5 %collective-permute-start.21 = (f32[2,1,16,128]{3,2,1,0:T(8,128)S(1)}, f32[2,1,16,128]{3,2,1,0:T(8,128)S(1)}, u32[]{:S(2)}, u32[]{:S(2)}) collective-permute-start(f32[2,1,16,128]{3,2,1,0:T(8,128)S(1)} %slice.1473), channel_id=1, source_target_pairs={{2,0},{4,2},{6,4},{8,6},{10,8},{12,10},{14,12},{3,1},{5,3},{7,5},{... | collective-permute-start | bytes 49160 | tf_op jit(solution)/shard_map/ppermute | solution.py:14
  164.6 7.1 %collective-permute-start.22 = (f32[2,16,1,128]{3,1,2,0:T(8,128)S(1)}, f32[2,16,1,128]{3,1,2,0:T(8,128)S(1)}, u32[]{:S(2)}, u32[]{:S(2)}) collective-permute-start(f32[2,16,1,128]{3,1,2,0:T(8,128)S(1)} %bitcast.597), channel_id=1, source_target_pairs={{0,1},{2,3},{4,5},{6,7},{8,9},{10,11},{12,13},{14,15},{16,17},{18,... | collective-permute-start | bytes 49160 | tf_op jit(solution)/shard_map/ppermute | solution.py:14
  166.0 6.3 %collective-permute-start.23 = (f32[2,1,16,128]{3,2,1,0:T(8,128)S(1)}, f32[2,1,16,128]{3,2,1,0:T(8,128)S(1)}, u32[]{:S(2)}, u32[]{:S(2)}) collective-permute-start(f32[2,1,16,128]{3,2,1,0:T(8,128)S(1)} %slice.1486), channel_id=1, source_target_pairs={{0,2},{2,4},{4,6},{6,8},{8,10},{10,12},{12,14},{1,3},{3,5},{5,7},{... | collective-permute-start | bytes 49160 | tf_op jit(solution)/shard_map/ppermute | solution.py:14
  180.8 7.1 %collective-permute-start.24 = (f32[2,16,1,128]{3,1,2,0:T(8,128)S(1)}, f32[2,16,1,128]{3,1,2,0:T(8,128)S(1)}, u32[]{:S(2)}, u32[]{:S(2)}) collective-permute-start(f32[2,16,1,128]{3,1,2,0:T(8,128)S(1)} %bitcast.591), channel_id=1, source_target_pairs={{1,0},{3,2},{5,4},{7,6},{9,8},{11,10},{13,12},{15,14},{17,16},{19,... | collective-permute-start | bytes 49160 | tf_op jit(solution)/shard_map/ppermute | solution.py:14
  186.4 6.5 %collective-permute-start.25 = (f32[2,1,16,128]{3,2,1,0:T(8,128)S(1)}, f32[2,1,16,128]{3,2,1,0:T(8,128)S(1)}, u32[]{:S(2)}, u32[]{:S(2)}) collective-permute-start(f32[2,1,16,128]{3,2,1,0:T(8,128)S(1)} %slice.1504), channel_id=1, source_target_pairs={{2,0},{4,2},{6,4},{8,6},{10,8},{12,10},{14,12},{3,1},{5,3},{7,5},{... | collective-permute-start | bytes 49160 | tf_op jit(solution)/shard_map/ppermute | solution.py:14
  194.6 7.1 %collective-permute-start.26 = (f32[2,16,1,128]{3,1,2,0:T(8,128)S(1)}, f32[2,16,1,128]{3,1,2,0:T(8,128)S(1)}, u32[]{:S(2)}, u32[]{:S(2)}) collective-permute-start(f32[2,16,1,128]{3,1,2,0:T(8,128)S(1)} %bitcast.598), channel_id=1, source_target_pairs={{0,1},{2,3},{4,5},{6,7},{8,9},{10,11},{12,13},{14,15},{16,17},{18,... | collective-permute-start | bytes 49160 | tf_op jit(solution)/shard_map/ppermute | solution.py:14
  195.9 6.3 %collective-permute-start.27 = (f32[2,1,16,128]{3,2,1,0:T(8,128)S(1)}, f32[2,1,16,128]{3,2,1,0:T(8,128)S(1)}, u32[]{:S(2)}, u32[]{:S(2)}) collective-permute-start(f32[2,1,16,128]{3,2,1,0:T(8,128)S(1)} %slice.1517), channel_id=1, source_target_pairs={{0,2},{2,4},{4,6},{6,8},{8,10},{10,12},{12,14},{1,3},{3,5},{5,7},{... | collective-permute-start | bytes 49160 | tf_op jit(solution)/shard_map/ppermute | solution.py:14
  210.9 6.9 %collective-permute-start.28 = (f32[2,16,1,128]{3,2,1,0:T(1,128)S(1)}, f32[2,16,1,128]{3,2,1,0:T(1,128)S(1)}, u32[]{:S(2)}, u32[]{:S(2)}) collective-permute-start(f32[2,16,1,128]{3,2,1,0:T(1,128)S(1)} %slice.1285), channel_id=1, source_target_pairs={{1,0},{3,2},{5,4},{7,6},{9,8},{11,10},{13,12},{15,14},{17,16},{19,... | collective-permute-start | bytes 49160 | tf_op jit(solution)/shard_map/ppermute | solution.py:14
  216.5 6.5 %collective-permute-start.29 = (f32[2,1,16,128]{3,2,1,0:T(8,128)S(1)}, f32[2,1,16,128]{3,2,1,0:T(8,128)S(1)}, u32[]{:S(2)}, u32[]{:S(2)}) collective-permute-start(f32[2,1,16,128]{3,2,1,0:T(8,128)S(1)} %slice.1535), channel_id=1, source_target_pairs={{2,0},{4,2},{6,4},{8,6},{10,8},{12,10},{14,12},{3,1},{5,3},{7,5},{... | collective-permute-start | bytes 49160 | tf_op jit(solution)/shard_map/ppermute | solution.py:14
  224.7 7.1 %collective-permute-start.30 = (f32[2,16,1,128]{3,1,2,0:T(8,128)S(1)}, f32[2,16,1,128]{3,1,2,0:T(8,128)S(1)}, u32[]{:S(2)}, u32[]{:S(2)}) collective-permute-start(f32[2,16,1,128]{3,1,2,0:T(8,128)S(1)} %bitcast.599), channel_id=1, source_target_pairs={{0,1},{2,3},{4,5},{6,7},{8,9},{10,11},{12,13},{14,15},{16,17},{18,... | collective-permute-start | bytes 49160 | tf_op jit(solution)/shard_map/ppermute | solution.py:14
  226.1 6.3 %collective-permute-start.31 = (f32[2,1,16,128]{3,2,1,0:T(8,128)S(1)}, f32[2,1,16,128]{3,2,1,0:T(8,128)S(1)}, u32[]{:S(2)}, u32[]{:S(2)}) collective-permute-start(f32[2,1,16,128]{3,2,1,0:T(8,128)S(1)} %slice.1548), channel_id=1, source_target_pairs={{0,2},{2,4},{4,6},{6,8},{8,10},{10,12},{12,14},{1,3},{3,5},{5,7},{... | collective-permute-start | bytes 49160 | tf_op jit(solution)/shard_map/ppermute | solution.py:14
  (83 other events, 139.9 us)
Sparse Core Ops, SparseCore 0:
  235.6 61.6 reduce-scatter.1
